TPU v7x, 128 devices: a whole 4x4x4 slice. The times are simulated.
128 devices in a mesh: rows: 32 (over y, z, core), feat: 4 (over x).
Axes of the slice: x: 4, y: 4, z: 4, core: 2. Of those that a mesh axis runs over, the one named last changes fastest.
Arguments:
- bin_codes: int32 [131072, 2048], P('rows', 'feat'), may hold values from 0 to 255
- gradient: bfloat16 [131072], P('rows'), may hold values from -6 to 6
- hessian: bfloat16 [131072], P('rows'), may hold values from 0.049804688 to 1
- leaf_of_block: int32 [1024], P('rows'), may hold values from 0 to 1
- block_rows: int32 [1024], P('rows'), may hold values from 32 to 128, as said below
Outputs:
- split_gain: float32 [2, 2048, 256], P(None, ('feat', 'rows'))
- best_gain: float32 [2], replicated
Inputs may be any that keep to these rules, and one draw needn't show every extreme that they name: `block_rows`: the live rows are the first ones of their block; some block is full in every draw.
All inputs are finite; a program needn't handle non-finite values.
Results may differ from a plain program's by a relative error of at most 0.0003.
Values sent between devices are 32-bit elements; how exact they have to be, the bound alone decides.
A program may use at most 64 MiB of HBM per device.

v0:
```python
import math

import jax
import jax.numpy as jnp
from jax import lax
from jax.sharding import PartitionSpec as P

BINS = 256
LEAVES = 2
BLOCK = 128
MIN_CHILD = 20


ridge_term = 1.0


def local(bin_codes, gradient, hessian, leaf_of_block, block_rows):
    row_total, feat_local = bin_codes.shape
    owners = lax.axis_size("rows")
    per_owner = feat_local // owners
    offsets = jnp.arange(row_total, dtype=jnp.int32) % BLOCK
    live_rows = (offsets < jnp.repeat(block_rows, BLOCK)).astype(jnp.float32)
    leaf_ids = jnp.repeat(leaf_of_block, BLOCK)
    leaf_hot = (leaf_ids[:, None] == jnp.arange(LEAVES, dtype=jnp.int32)[None, :]).astype(
        jnp.float32
    ) * live_rows[:, None]
    weights = jnp.concatenate(
        [
            gradient.astype(jnp.float32)[:, None] * leaf_hot,
            hessian.astype(jnp.float32)[:, None] * leaf_hot,
            leaf_hot,
        ],
        1,
    ).astype(jnp.bfloat16)
    bin_values = jnp.arange(BINS, dtype=jnp.int32)
    sub_width = math.gcd(per_owner * lax.axis_size("rows"), 16)

    def sub_block(block_index):
        code_slice = lax.dynamic_slice_in_dim(bin_codes, block_index * sub_width, sub_width, 1)
        onehot = (code_slice[:, :, None] == bin_values).astype(jnp.bfloat16)
        block_sums = jnp.einsum("rs,rwb->wsb", weights, onehot, preferred_element_type=jnp.float32)
        return block_sums.reshape(sub_width, 3, LEAVES, BINS)

    stacked = lax.map(
        sub_block, jnp.arange(per_owner * lax.axis_size("rows") // sub_width, dtype=jnp.int32)
    )
    histogram = lax.psum_scatter(
        stacked.reshape(per_owner * lax.axis_size("rows"), 3, LEAVES, BINS),
        "rows",
        scatter_dimension=0,
        tiled=True,
    )
    running = jnp.cumsum(histogram, axis=3)
    totals = running[..., -1:]
    left_grad, left_hess, left_count = (running[:, 0], running[:, 1], running[:, 2])
    total_grad, total_hess, total_count = (totals[:, 0], totals[:, 1], totals[:, 2])
    right_grad = total_grad - left_grad
    right_hess = total_hess - left_hess
    right_count = total_count - left_count
    raw_gain = 0.5 * (
        left_grad**2 / (left_hess + ridge_term)
        + right_grad**2 / (right_hess + ridge_term)
        - total_grad**2 / (total_hess + ridge_term)
    )
    allowed = (left_count >= MIN_CHILD) & (right_count >= MIN_CHILD)
    split_gain = jnp.transpose(jnp.where(allowed, raw_gain, 0.0), (1, 0, 2))
    best_local = jnp.max(split_gain, axis=(1, 2))
    best_gain = lax.pmax(best_local, ("rows", "feat"))
    return (split_gain, best_gain)


def solution(mesh):
    return jax.shard_map(
        local,
        mesh=mesh,
        in_specs=(P("rows", "feat"), P("rows"), P("rows"), P("rows"), P("rows")),
        out_specs=(P(None, ("feat", "rows"), None), P()),
        check_vma=False,
    )
```

profile of v0, /device:TPU:1, one launch (start us, length us, event | category | flops | bytes accessed | tf_op | source)
XLA Modules:
  0.0 685.8 jit_solution(8709033014641565480)
XLA Ops:
  19.1 506.0 %while.11 = (s32[]{:T(128)}, f32[32,16,3,2,256]{4,1,0,3,2:T(8,128)}, s32[32]{0:T(128)S(1)}, s32[4096,512]{0,1:T(8,128)}, bf16[4096,6]{0,1:T(8,128)(2,1)S(1)}, /*...) while((s32[]{:T(128)}, f32[32,16,3,2,256]{4,1,0,3,2:T(8,128)}, s32[32]{0:T(128)S(1)}, ...), condition=%wide.region_1.2_spmd.clone, body=%wide.region_0.1_spmd.clone.sunk | while | flops 218103808 | bytes 1327771 | solution.py:44
  21.3 12.9 %fusion.19 = f32[16,6,256]{2,1,0:T(8,128)S(1)} fusion(s32[4096,16]{0,1:T(8,128)S(1)} %constant_dynamic-slice_fusion.2, bf16[4096,6]{0,1:T(8,128)(2,1)S(1)} %get-tuple-element.132), kind=kOutput, calls=%fused_computation.4.clone.2 | convolution fusion | flops 218103808 | bytes 409600 | tf_op jit(solution)/shard_map/while/body/eval_jaxpr/rs,rwb->wsb/dot_general | solution.py:41
  37.2 12.9 %fusion.19 = f32[16,6,256]{2,1,0:T(8,128)S(1)} fusion(s32[4096,16]{0,1:T(8,128)S(1)} %constant_dynamic-slice_fusion.2, bf16[4096,6]{0,1:T(8,128)(2,1)S(1)} %get-tuple-element.132), kind=kOutput, calls=%fused_computation.4.clone.2 | convolution fusion | flops 218103808 | bytes 409600 | tf_op jit(solution)/shard_map/while/body/eval_jaxpr/rs,rwb->wsb/dot_general | solution.py:41
  53.0 12.9 %fusion.19 = f32[16,6,256]{2,1,0:T(8,128)S(1)} fusion(s32[4096,16]{0,1:T(8,128)S(1)} %constant_dynamic-slice_fusion.2, bf16[4096,6]{0,1:T(8,128)(2,1)S(1)} %get-tuple-element.132), kind=kOutput, calls=%fused_computation.4.clone.2 | convolution fusion | flops 218103808 | bytes 409600 | tf_op jit(solution)/shard_map/while/body/eval_jaxpr/rs,rwb->wsb/dot_general | solution.py:41
  68.8 12.9 %fusion.19 = f32[16,6,256]{2,1,0:T(8,128)S(1)} fusion(s32[4096,16]{0,1:T(8,128)S(1)} %constant_dynamic-slice_fusion.2, bf16[4096,6]{0,1:T(8,128)(2,1)S(1)} %get-tuple-element.132), kind=kOutput, calls=%fused_computation.4.clone.2 | convolution fusion | flops 218103808 | bytes 409600 | tf_op jit(solution)/shard_map/while/body/eval_jaxpr/rs,rwb->wsb/dot_general | solution.py:41
  84.6 12.9 %fusion.19 = f32[16,6,256]{2,1,0:T(8,128)S(1)} fusion(s32[4096,16]{0,1:T(8,128)S(1)} %constant_dynamic-slice_fusion.2, bf16[4096,6]{0,1:T(8,128)(2,1)S(1)} %get-tuple-element.132), kind=kOutput, calls=%fused_computation.4.clone.2 | convolution fusion | flops 218103808 | bytes 409600 | tf_op jit(solution)/shard_map/while/body/eval_jaxpr/rs,rwb->wsb/dot_general | solution.py:41
  100.4 12.9 %fusion.19 = f32[16,6,256]{2,1,0:T(8,128)S(1)} fusion(s32[4096,16]{0,1:T(8,128)S(1)} %constant_dynamic-slice_fusion.2, bf16[4096,6]{0,1:T(8,128)(2,1)S(1)} %get-tuple-element.132), kind=kOutput, calls=%fused_computation.4.clone.2 | convolution fusion | flops 218103808 | bytes 409600 | tf_op jit(solution)/shard_map/while/body/eval_jaxpr/rs,rwb->wsb/dot_general | solution.py:41
  116.2 12.9 %fusion.19 = f32[16,6,256]{2,1,0:T(8,128)S(1)} fusion(s32[4096,16]{0,1:T(8,128)S(1)} %constant_dynamic-slice_fusion.2, bf16[4096,6]{0,1:T(8,128)(2,1)S(1)} %get-tuple-element.132), kind=kOutput, calls=%fused_computation.4.clone.2 | convolution fusion | flops 218103808 | bytes 409600 | tf_op jit(solution)/shard_map/while/body/eval_jaxpr/rs,rwb->wsb/dot_general | solution.py:41
  132.0 12.9 %fusion.19 = f32[16,6,256]{2,1,0:T(8,128)S(1)} fusion(s32[4096,16]{0,1:T(8,128)S(1)} %constant_dynamic-slice_fusion.2, bf16[4096,6]{0,1:T(8,128)(2,1)S(1)} %get-tuple-element.132), kind=kOutput, calls=%fused_computation.4.clone.2 | convolution fusion | flops 218103808 | bytes 409600 | tf_op jit(solution)/shard_map/while/body/eval_jaxpr/rs,rwb->wsb/dot_general | solution.py:41
  147.8 12.9 %fusion.19 = f32[16,6,256]{2,1,0:T(8,128)S(1)} fusion(s32[4096,16]{0,1:T(8,128)S(1)} %constant_dynamic-slice_fusion.2, bf16[4096,6]{0,1:T(8,128)(2,1)S(1)} %get-tuple-element.132), kind=kOutput, calls=%fused_computation.4.clone.2 | convolution fusion | flops 218103808 | bytes 409600 | tf_op jit(solution)/shard_map/while/body/eval_jaxpr/rs,rwb->wsb/dot_general | solution.py:41
  163.6 12.9 %fusion.19 = f32[16,6,256]{2,1,0:T(8,128)S(1)} fusion(s32[4096,16]{0,1:T(8,128)S(1)} %constant_dynamic-slice_fusion.2, bf16[4096,6]{0,1:T(8,128)(2,1)S(1)} %get-tuple-element.132), kind=kOutput, calls=%fused_computation.4.clone.2 | convolution fusion | flops 218103808 | bytes 409600 | tf_op jit(solution)/shard_map/while/body/eval_jaxpr/rs,rwb->wsb/dot_general | solution.py:41
  179.4 12.9 %fusion.19 = f32[16,6,256]{2,1,0:T(8,128)S(1)} fusion(s32[4096,16]{0,1:T(8,128)S(1)} %constant_dynamic-slice_fusion.2, bf16[4096,6]{0,1:T(8,128)(2,1)S(1)} %get-tuple-element.132), kind=kOutput, calls=%fused_computation.4.clone.2 | convolution fusion | flops 218103808 | bytes 409600 | tf_op jit(solution)/shard_map/while/body/eval_jaxpr/rs,rwb->wsb/dot_general | solution.py:41
  195.2 12.9 %fusion.19 = f32[16,6,256]{2,1,0:T(8,128)S(1)} fusion(s32[4096,16]{0,1:T(8,128)S(1)} %constant_dynamic-slice_fusion.2, bf16[4096,6]{0,1:T(8,128)(2,1)S(1)} %get-tuple-element.132), kind=kOutput, calls=%fused_computation.4.clone.2 | convolution fusion | flops 218103808 | bytes 409600 | tf_op jit(solution)/shard_map/while/body/eval_jaxpr/rs,rwb->wsb/dot_general | solution.py:41
  211.0 12.9 %fusion.19 = f32[16,6,256]{2,1,0:T(8,128)S(1)} fusion(s32[4096,16]{0,1:T(8,128)S(1)} %constant_dynamic-slice_fusion.2, bf16[4096,6]{0,1:T(8,128)(2,1)S(1)} %get-tuple-element.132), kind=kOutput, calls=%fused_computation.4.clone.2 | convolution fusion | flops 218103808 | bytes 409600 | tf_op jit(solution)/shard_map/while/body/eval_jaxpr/rs,rwb->wsb/dot_general | solution.py:41
  226.9 12.9 %fusion.19 = f32[16,6,256]{2,1,0:T(8,128)S(1)} fusion(s32[4096,16]{0,1:T(8,128)S(1)} %constant_dynamic-slice_fusion.2, bf16[4096,6]{0,1:T(8,128)(2,1)S(1)} %get-tuple-element.132), kind=kOutput, calls=%fused_computation.4.clone.2 | convolution fusion | flops 218103808 | bytes 409600 | tf_op jit(solution)/shard_map/while/body/eval_jaxpr/rs,rwb->wsb/dot_general | solution.py:41
  242.7 12.9 %fusion.19 = f32[16,6,256]{2,1,0:T(8,128)S(1)} fusion(s32[4096,16]{0,1:T(8,128)S(1)} %constant_dynamic-slice_fusion.2, bf16[4096,6]{0,1:T(8,128)(2,1)S(1)} %get-tuple-element.132), kind=kOutput, calls=%fused_computation.4.clone.2 | convolution fusion | flops 218103808 | bytes 409600 | tf_op jit(solution)/shard_map/while/body/eval_jaxpr/rs,rwb->wsb/dot_general | solution.py:41
  258.5 12.9 %fusion.19 = f32[16,6,256]{2,1,0:T(8,128)S(1)} fusion(s32[4096,16]{0,1:T(8,128)S(1)} %constant_dynamic-slice_fusion.2, bf16[4096,6]{0,1:T(8,128)(2,1)S(1)} %get-tuple-element.132), kind=kOutput, calls=%fused_computation.4.clone.2 | convolution fusion | flops 218103808 | bytes 409600 | tf_op jit(solution)/shard_map/while/body/eval_jaxpr/rs,rwb->wsb/dot_general | solution.py:41
  274.3 12.9 %fusion.19 = f32[16,6,256]{2,1,0:T(8,128)S(1)} fusion(s32[4096,16]{0,1:T(8,128)S(1)} %constant_dynamic-slice_fusion.2, bf16[4096,6]{0,1:T(8,128)(2,1)S(1)} %get-tuple-element.132), kind=kOutput, calls=%fused_computation.4.clone.2 | convolution fusion | flops 218103808 | bytes 409600 | tf_op jit(solution)/shard_map/while/body/eval_jaxpr/rs,rwb->wsb/dot_general | solution.py:41
  290.2 12.9 %fusion.19 = f32[16,6,256]{2,1,0:T(8,128)S(1)} fusion(s32[4096,16]{0,1:T(8,128)S(1)} %constant_dynamic-slice_fusion.2, bf16[4096,6]{0,1:T(8,128)(2,1)S(1)} %get-tuple-element.132), kind=kOutput, calls=%fused_computation.4.clone.2 | convolution fusion | flops 218103808 | bytes 409600 | tf_op jit(solution)/shard_map/while/body/eval_jaxpr/rs,rwb->wsb/dot_general | solution.py:41
  306.0 12.9 %fusion.19 = f32[16,6,256]{2,1,0:T(8,128)S(1)} fusion(s32[4096,16]{0,1:T(8,128)S(1)} %constant_dynamic-slice_fusion.2, bf16[4096,6]{0,1:T(8,128)(2,1)S(1)} %get-tuple-element.132), kind=kOutput, calls=%fused_computation.4.clone.2 | convolution fusion | flops 218103808 | bytes 409600 | tf_op jit(solution)/shard_map/while/body/eval_jaxpr/rs,rwb->wsb/dot_general | solution.py:41
  321.8 12.9 %fusion.19 = f32[16,6,256]{2,1,0:T(8,128)S(1)} fusion(s32[4096,16]{0,1:T(8,128)S(1)} %constant_dynamic-slice_fusion.2, bf16[4096,6]{0,1:T(8,128)(2,1)S(1)} %get-tuple-element.132), kind=kOutput, calls=%fused_computation.4.clone.2 | convolution fusion | flops 218103808 | bytes 409600 | tf_op jit(solution)/shard_map/while/body/eval_jaxpr/rs,rwb->wsb/dot_general | solution.py:41
  337.7 12.9 %fusion.19 = f32[16,6,256]{2,1,0:T(8,128)S(1)} fusion(s32[4096,16]{0,1:T(8,128)S(1)} %constant_dynamic-slice_fusion.2, bf16[4096,6]{0,1:T(8,128)(2,1)S(1)} %get-tuple-element.132), kind=kOutput, calls=%fused_computation.4.clone.2 | convolution fusion | flops 218103808 | bytes 409600 | tf_op jit(solution)/shard_map/while/body/eval_jaxpr/rs,rwb->wsb/dot_general | solution.py:41
  353.5 12.9 %fusion.19 = f32[16,6,256]{2,1,0:T(8,128)S(1)} fusion(s32[4096,16]{0,1:T(8,128)S(1)} %constant_dynamic-slice_fusion.2, bf16[4096,6]{0,1:T(8,128)(2,1)S(1)} %get-tuple-element.132), kind=kOutput, calls=%fused_computation.4.clone.2 | convolution fusion | flops 218103808 | bytes 409600 | tf_op jit(solution)/shard_map/while/body/eval_jaxpr/rs,rwb->wsb/dot_general | solution.py:41
  369.3 12.9 %fusion.19 = f32[16,6,256]{2,1,0:T(8,128)S(1)} fusion(s32[4096,16]{0,1:T(8,128)S(1)} %constant_dynamic-slice_fusion.2, bf16[4096,6]{0,1:T(8,128)(2,1)S(1)} %get-tuple-element.132), kind=kOutput, calls=%fused_computation.4.clone.2 | convolution fusion | flops 218103808 | bytes 409600 | tf_op jit(solution)/shard_map/while/body/eval_jaxpr/rs,rwb->wsb/dot_general | solution.py:41
  385.1 12.9 %fusion.19 = f32[16,6,256]{2,1,0:T(8,128)S(1)} fusion(s32[4096,16]{0,1:T(8,128)S(1)} %constant_dynamic-slice_fusion.2, bf16[4096,6]{0,1:T(8,128)(2,1)S(1)} %get-tuple-element.132), kind=kOutput, calls=%fused_computation.4.clone.2 | convolution fusion | flops 218103808 | bytes 409600 | tf_op jit(solution)/shard_map/while/body/eval_jaxpr/rs,rwb->wsb/dot_general | solution.py:41
  400.9 12.9 %fusion.19 = f32[16,6,256]{2,1,0:T(8,128)S(1)} fusion(s32[4096,16]{0,1:T(8,128)S(1)} %constant_dynamic-slice_fusion.2, bf16[4096,6]{0,1:T(8,128)(2,1)S(1)} %get-tuple-element.132), kind=kOutput, calls=%fused_computation.4.clone.2 | convolution fusion | flops 218103808 | bytes 409600 | tf_op jit(solution)/shard_map/while/body/eval_jaxpr/rs,rwb->wsb/dot_general | solution.py:41
  416.7 12.9 %fusion.19 = f32[16,6,256]{2,1,0:T(8,128)S(1)} fusion(s32[4096,16]{0,1:T(8,128)S(1)} %constant_dynamic-slice_fusion.2, bf16[4096,6]{0,1:T(8,128)(2,1)S(1)} %get-tuple-element.132), kind=kOutput, calls=%fused_computation.4.clone.2 | convolution fusion | flops 218103808 | bytes 409600 | tf_op jit(solution)/shard_map/while/body/eval_jaxpr/rs,rwb->wsb/dot_general | solution.py:41
  432.5 12.9 %fusion.19 = f32[16,6,256]{2,1,0:T(8,128)S(1)} fusion(s32[4096,16]{0,1:T(8,128)S(1)} %constant_dynamic-slice_fusion.2, bf16[4096,6]{0,1:T(8,128)(2,1)S(1)} %get-tuple-element.132), kind=kOutput, calls=%fused_computation.4.clone.2 | convolution fusion | flops 218103808 | bytes 409600 | tf_op jit(solution)/shard_map/while/body/eval_jaxpr/rs,rwb->wsb/dot_general | solution.py:41
  448.3 12.9 %fusion.19 = f32[16,6,256]{2,1,0:T(8,128)S(1)} fusion(s32[4096,16]{0,1:T(8,128)S(1)} %constant_dynamic-slice_fusion.2, bf16[4096,6]{0,1:T(8,128)(2,1)S(1)} %get-tuple-element.132), kind=kOutput, calls=%fused_computation.4.clone.2 | convolution fusion | flops 218103808 | bytes 409600 | tf_op jit(solution)/shard_map/while/body/eval_jaxpr/rs,rwb->wsb/dot_general | solution.py:41
  479.9 12.9 %fusion.19 = f32[16,6,256]{2,1,0:T(8,128)S(1)} fusion(s32[4096,16]{0,1:T(8,128)S(1)} %constant_dynamic-slice_fusion.2, bf16[4096,6]{0,1:T(8,128)(2,1)S(1)} %get-tuple-element.132), kind=kOutput, calls=%fused_computation.4.clone.2 | convolution fusion | flops 218103808 | bytes 409600 | tf_op jit(solution)/shard_map/while/body/eval_jaxpr/rs,rwb->wsb/dot_general | solution.py:41
  525.2 82.3 %reduce-scatter.2.cloned.1.call-done = f32[16,3,2,256]{3,0,2,1:T(8,128)} async-done(((f32[512,3,2,256]{3,0,2,1:T(8,128)}), f32[16,3,2,256]{3,0,2,1:T(8,128)}) %reduce-scatter.2.cloned.1.call-update) | async-done | bytes 98320 | tf_op jit(solution)/shard_map/reduce_scatter | solution.py:47
  613.1 65.8 %pmax.7 = f32[2]{0:T(128)} all-reduce(f32[2]{0:T(128)S(1)} %get-tuple-element.75), channel_id=1, replica_groups=mesh['rows'=32,'feat'=4] {'rows','feat'}, use_global_device_ids=true, to_apply=%region_6.7 | all-reduce | flops 2 | bytes 16 | tf_op jit(solution)/shard_map/pmax | solution.py:68
  (156 shorter events, 128.5 us)
Async XLA Ops:
  7.2 0.7 copy-start
  7.2 600.3 %reduce-scatter.2.cloned.1.call-start = ((), (), s32[]{:S(2)}) async-start(), calls=%async_computation.1 | async-start | bytes 3244032 | tf_op jit(solution)/shard_map/reduce_scatter | solution.py:47
Sparse Core Ops, SparseCore 0:
  525.3 82.1 reduce-scatter.1
where the time goes:
time: 688 us; the launch traced here: 686 us
  matrix products  412 us (60%)
  local copies, waits for them, and re-layouts  83.3 us (12%)
  waiting for transfers between devices  82.3 us (12%)
  blocking collectives  65.8 us (10%)
  loops' own time  21.4 us (3%)
  between operations  14.1 us (2%)
    dot_general x32, matrix products, sub_block(): jnp.einsum('rs,rwb->wsb', weights, onehot, preferred_element_type=jnp.flo...  412 us
    reduce_scatter x1, waiting for transfers between devices, local(): lax.psum_scatter(stacked.reshape(per_owner * lax.axis_size('rows'), 3, LE...  82.3 us
    pmax x1, blocking collectives, local(): best_gain = lax.pmax(best_local, ('rows', 'feat'))  65.8 us
    dynamic_slice x32, local copies, waits for them, and re-layouts, sub_block(): lax.dynamic_slice_in_dim(bin_codes, block_index * sub_width, sub_width, 1)  31.1 us
    another operation x1, loops' own time, local(): lax.map(sub_block, jnp.arange(per_owner * lax.axis_size('rows') // sub_wi...  21.4 us
    dynamic_update_slice x32, local copies, waits for them, and re-layouts, local(): lax.map(sub_block, jnp.arange(per_owner * lax.axis_size('rows') // sub_wi...  21.2 us
    dynamic_slice x32, local copies, waits for them, and re-layouts, local(): lax.map(sub_block, jnp.arange(per_owner * lax.axis_size('rows') // sub_wi...  18.6 us
  transfers between devices with their start and end apart: 1, of which 1 were waited for; matrix products, arithmetic and copies ran while one was open for 0% of the time, Pallas kernels for 0%

commit v1 on v0

v1 whole, which is shorter than its diff:
```python
import functools
import jax
import jax.numpy as jnp
from jax import lax
from jax.experimental import pallas as pl
from jax.experimental.pallas import tpu as pltpu
from jax._src.pallas.mosaic.core import AccMemorySpace
from jax.sharding import PartitionSpec as P

BINS = 256
BLOCK = 128
LO = 32
HI = 8
FSTEP = 128
GROUP = 8


def hist_kernel(leaf_ref, live_ref, codes_ref, grad_ref, hess_ref, out_ref,
                compact, lo_ref, hi_ref, pair_ref, ones_ref, stat_ref, gf, hf):
    blocks = leaf_ref.shape[0]
    tiles = lo_ref.shape[0]
    first = pl.program_id(0) == 0

    def count(k, c):
        n = (live_ref[k] + 7) // 8 * 8
        one = leaf_ref[k]
        return c[0] + n * (1 - one), c[1] + n * one

    rows0, rows1 = lax.fori_loop(0, blocks, count, (jnp.int32(0), jnp.int32(0)))
    tiles0 = (rows0 + 255) // 256
    tiles1 = (rows1 + 255) // 256
    base1 = tiles0 * 256

    @pl.when(first)
    def _():
        gf[...] = grad_ref[...].astype(jnp.float32)
        hf[...] = hess_ref[...].astype(jnp.float32)
        stat_ref[...] = jnp.zeros_like(stat_ref)
        lane = lax.broadcasted_iota(jnp.int32, (8, 128), 1)
        sub = lax.broadcasted_iota(jnp.int32, (8, 128), 0)

        def place(k, off):
            n = live_ref[k]
            g = jnp.broadcast_to(gf[pl.ds(k, 1), :], (8, 128))
            h = jnp.broadcast_to(hf[pl.ds(k, 1), :], (8, 128))
            s = jnp.where(sub == 0, g, jnp.where(sub == 1, h, jnp.where(sub == 2, 1.0, 0.0)))
            s = jnp.where(lane < n, s, 0.0)
            shift = off % 128
            rolled = pltpu.roll(s, shift, 1)
            at = off // 128
            stat_ref[at] += jnp.where(lane >= shift, rolled, 0.0)
            stat_ref[at + 1] += jnp.where(lane < shift, rolled, 0.0)
            return off + (n + 7) // 8 * 8

        def pick(leaf, k, off):
            return lax.cond(leaf_ref[k] == leaf, lambda: place(k, off), lambda: off)

        lax.fori_loop(0, blocks, functools.partial(pick, 0), jnp.int32(0))
        lax.fori_loop(0, blocks, functools.partial(pick, 1), base1)

        @pl.loop(0, tiles)
        def _(t):
            for half in range(2):
                s = stat_ref[2 * t + half]
                g, h, c = (jnp.broadcast_to(s[i:i + 1, :], (8, 128)) for i in range(3))
                pair_ref[t, :, half * 128:half * 128 + 128] = jnp.concatenate([g, h], 0).astype(jnp.bfloat16)
                ones_ref[t, :, half * 128:half * 128 + 128] = jnp.concatenate([c, c], 0).astype(jnp.bfloat16)

    def move(leaf, k, off):
        def go():
            at = pl.multiple_of(off, 8)
            compact[pl.ds(at, BLOCK), :] = codes_ref[pl.ds(pl.multiple_of(k * BLOCK, BLOCK), BLOCK), :]
            return off + (live_ref[k] + 7) // 8 * 8
        return lax.cond(leaf_ref[k] == leaf, go, lambda: off)

    lax.fori_loop(0, blocks, functools.partial(move, 0), jnp.int32(0))
    lax.fori_loop(0, blocks, functools.partial(move, 1), base1)

    @pl.loop(0, (tiles0 + tiles1 + 1) // 2)
    def _(u):
        at = pl.multiple_of(u * 512, 512)
        word = compact[pl.ds(at, 128), :] & 255
        for q in range(1, 4):
            word = word | ((compact[pl.ds(at + 128 * q, 128), :] & 255) << (8 * q))
        word = word.T
        for q in range(4):
            lo = (word >> (8 * q)) & (LO - 1)
            hi = (word >> (8 * q + 5)) & (HI - 1)
            lanes = slice(128 * (q % 2), 128 * (q % 2) + 128)
            lo_ref[2 * u + q // 2, :, lanes] = lo.astype(jnp.float32)
            hi_ref[2 * u + q // 2, :, lanes] = hi.astype(jnp.float32)

    sub16 = lax.broadcasted_iota(jnp.int32, (16, 256), 0)
    lo_a = sub16.astype(jnp.float32).astype(jnp.bfloat16)
    lo_b = (sub16 + 16).astype(jnp.float32).astype(jnp.bfloat16)
    hi_n = (sub16 % 8).astype(jnp.float32).astype(jnp.bfloat16)
    one = jnp.ones((16, 256), jnp.bfloat16)
    zero = jnp.zeros((16, 256), jnp.bfloat16)
    lane_group = lax.broadcasted_iota(jnp.int32, (8, 128), 1) // LO

    groups = 8
    for leaf in range(2):
        for part in range(FSTEP // (groups * GROUP)):
            def run(*accs, leaf=leaf, part=part):
                def step(t, carry):
                    pair = pair_ref[t]
                    ones = ones_ref[t]
                    for i in range(groups):
                        rhs, lhs = [], []
                        for f2 in range(0, GROUP, 2):
                            his = []
                            for d in range(2):
                                f = part * groups * GROUP + i * GROUP + f2 + d
                                low = jnp.broadcast_to(lo_ref[t, f:f + 1, :], (16, 256)).astype(jnp.bfloat16)
                                rhs.append(jnp.where(low == lo_a, one, zero))
                                rhs.append(jnp.where(low == lo_b, one, zero))
                                high = jnp.broadcast_to(hi_ref[t, f:f + 1, :], (8, 256))
                                his.append(high)
                                high = jnp.concatenate([high, high], 0).astype(jnp.bfloat16)
                                lhs.append(jnp.where(high == hi_n, pair, zero))
                            both = jnp.concatenate(his, 0).astype(jnp.bfloat16)
                            lhs.append(jnp.where(both == hi_n, ones, zero))
                        stage = (i // 2) % 2
                        pltpu.matmul_push_rhs(jnp.concatenate(rhs, 0), stage, i % 2, transpose=True)
                        pltpu.matmul_acc_lhs(accs[i], jnp.concatenate(lhs, 0), load_staged_rhs=stage)
                    return carry

                lo_t = 0 if leaf == 0 else tiles0
                hi_t = tiles0 if leaf == 0 else tiles0 + tiles1
                lax.fori_loop(lo_t, hi_t, step, 0)
                for i in range(groups):
                    sums = pltpu.matmul_pop(accs[i])
                    for q in range(2):
                        for s in range(3):
                            tile = None
                            for d in range(4):
                                f = 4 * q + d
                                row = 48 * (f // 2) + (16 * (f % 2) + 8 * s if s < 2 else 32 + 8 * (f % 2))
                                piece = sums[row:row + 8, 128 * q:128 * q + 128]
                                tile = piece if tile is None else jnp.where(lane_group == d, piece, tile)
                            gq = (part * groups + i) * 2 + q
                            out_ref[gq // 4, leaf, gq % 4, s] = tile

            pl.run_scoped(run, *[AccMemorySpace(i % 2)((24 * GROUP, 256), jnp.float32) for i in range(groups)])


def local_hist(codes, grad, hess, leaf, live):
    rows, feats = codes.shape
    blocks = leaf.shape[0]
    tiles = rows // 256 + 2
    owners = FSTEP // 16
    spec = pltpu.PrefetchScalarGridSpec(
        num_scalar_prefetch=2,
        grid=(feats // FSTEP,),
        in_specs=[
            pl.BlockSpec((rows, FSTEP), lambda i, *_: (0, i)),
            pl.BlockSpec((blocks, BLOCK), lambda i, *_: (0, 0)),
            pl.BlockSpec((blocks, BLOCK), lambda i, *_: (0, 0)),
        ],
        out_specs=pl.BlockSpec((owners, 2, 4, 3, 8, 128), lambda i, *_: (i, 0, 0, 0, 0, 0)),
        scratch_shapes=[
            pltpu.VMEM((tiles * 256 + BLOCK, FSTEP), jnp.int32),
            pltpu.VMEM((tiles, FSTEP, 256), jnp.float32),
            pltpu.VMEM((tiles, FSTEP, 256), jnp.float32),
            pltpu.VMEM((tiles, 16, 256), jnp.bfloat16),
            pltpu.VMEM((tiles, 16, 256), jnp.bfloat16),
            pltpu.VMEM((2 * tiles + 1, 8, 128), jnp.float32),
            pltpu.VMEM((blocks, BLOCK), jnp.float32),
            pltpu.VMEM((blocks, BLOCK), jnp.float32),
        ],
    )
    return pl.pallas_call(
        hist_kernel,
        out_shape=jax.ShapeDtypeStruct((feats // 16, 2, 4, 3, 8, 128), jnp.float32),
        grid_spec=spec,
        name="histogram",
        compiler_params=pltpu.CompilerParams(vmem_limit_bytes=48 << 20),
    )(leaf, live, codes, grad.reshape(blocks, BLOCK), hess.reshape(blocks, BLOCK))


MIN_CHILD = 20
ridge_term = 1.0


def local(bin_codes, gradient, hessian, leaf_of_block, block_rows):
    mine = local_hist(bin_codes, gradient, hessian, leaf_of_block, block_rows)
    mine = lax.psum_scatter(mine, "rows", scatter_dimension=0, tiled=True)
    histogram = mine.reshape(2, 4, 3, HI, 4, LO).transpose(1, 4, 2, 0, 3, 5).reshape(16, 3, 2, BINS)
    running = jnp.cumsum(histogram, axis=3)
    totals = running[..., -1:]
    left_grad, left_hess, left_count = (running[:, 0], running[:, 1], running[:, 2])
    total_grad, total_hess, total_count = (totals[:, 0], totals[:, 1], totals[:, 2])
    right_grad = total_grad - left_grad
    right_hess = total_hess - left_hess
    right_count = total_count - left_count
    raw_gain = 0.5 * (
        left_grad**2 / (left_hess + ridge_term)
        + right_grad**2 / (right_hess + ridge_term)
        - total_grad**2 / (total_hess + ridge_term)
    )
    allowed = (left_count >= MIN_CHILD) & (right_count >= MIN_CHILD)
    split_gain = jnp.transpose(jnp.where(allowed, raw_gain, 0.0), (1, 0, 2))
    best_gain = lax.pmax(jnp.max(split_gain, axis=(1, 2)), ("rows", "feat"))
    return (split_gain, best_gain)


def solution(mesh):
    return jax.shard_map(
        local,
        mesh=mesh,
        in_specs=(P("rows", "feat"), P("rows"), P("rows"), P("rows"), P("rows")),
        out_specs=(P(None, ("feat", "rows"), None), P()),
        check_vma=False,
    )
```

time: 688 us -> 229 us (0.33)
  matrix products: 412 us -> 0 us
  local copies, waits for them, and re-layouts: 83.3 us -> 4.41 us
  Pallas kernels: 0 us -> 54.1 us
  loops' own time: 21.4 us -> 0 us
    dot_general x32 -> x0, matrix products: 412 us -> none  [sub_block(): jnp.einsum('rs,rwb->wsb', weights, onehot, preferred_element_type=jnp.flo...]
    pallas_call x0 -> x1, Pallas kernels: none -> 54.1 us  [local_hist(): pl.pallas_call(hist_kernel, out_shape=jax.ShapeDtypeStruct((feats // 16,...]
    dynamic_slice x64 -> x0, local copies, waits for them, and re-layouts: 49.8 us -> none  [the longest x32 31.1 us: sub_block(): lax.dynamic_slice_in_dim(bin_codes, block_index * sub_width, sub_width, 1)]
    another operation x1 -> x0, loops' own time: 21.4 us -> none  [local(): lax.map(sub_block, jnp.arange(per_owner * lax.axis_size('rows') // sub_wi...]
    dynamic_update_slice x32 -> x0, local copies, waits for them, and re-layouts: 21.2 us -> none  [local(): lax.map(sub_block, jnp.arange(per_owner * lax.axis_size('rows') // sub_wi...]
where the time goes in v1:
time: 229 us; the launch traced here: 225 us
  waiting for transfers between devices  82.3 us (36%)
  blocking collectives  65.8 us (29%)
  Pallas kernels  54.1 us (24%)
  between operations  14.1 us (6%)
  local copies, waits for them, and re-layouts  4.41 us (2%)
  other arithmetic  4.28 us (2%)
    reduce_scatter x1, waiting for transfers between devices, local(): mine = lax.psum_scatter(mine, 'rows', scatter_dimension=0, tiled=True)  82.3 us
    pmax x1, blocking collectives, local(): best_gain = lax.pmax(jnp.max(split_gain, axis=(1, 2)), ('rows', 'feat'))  65.8 us
    pallas_call x1, Pallas kernels, local_hist(): pl.pallas_call(hist_kernel, out_shape=jax.ShapeDtypeStruct((feats // 16,...  54.1 us
  transfers between devices with their start and end apart: 1, of which 1 were waited for; matrix products, arithmetic and copies ran while one was open for 0% of the time, Pallas kernels for 0%

profile of v1, /device:TPU:1, one launch (start us, length us, event | category | flops | bytes accessed | tf_op | source)
XLA Modules:
  0.0 225.1 jit_solution(18338923430845624343)
XLA Ops:
  7.2 0.0 reduce-scatter.2.cloned.1.call-start
  7.2 0.0 copy-start
  7.2 0.7 copy-done
  7.9 0.0 copy-start.1
  7.9 0.7 copy-done.1
  8.6 0.0 copy-start.2
  8.6 0.7 copy-done.2
  9.3 0.0 copy-start.3
  9.3 0.7 copy-done.3
  9.9 54.1 %histogram.1 = f32[32,2,4,3,8,128]{5,4,3,2,1,0:T(8,128)} custom-call(s32[32]{0:T(128)S(1)} %copy-done.2, s32[32]{0:T(128)S(1)} %copy-done.3, s32[4096,512]{1,0:T(8,128)} %codes_ref.1, bf16[32,128]{1,0:T(8,128)(2,1)S(1)} %bitcast.31, bf16[32,128]{1,0:T(8,128)(2,1)S(1)} %bitcast.32), custom_call_target="tpu_custom_call" | custom-call | tf_op jit(solution)/shard_map/histogram/pallas_call | solution.py:172
  64.0 0.0 reduce-scatter.2.cloned.1.call-update
  64.0 82.3 %reduce-scatter.2.cloned.1.call-done = f32[1,2,4,3,8,128]{5,4,3,2,1,0:T(8,128)} async-done(((f32[32,2,4,3,8,128]{5,4,3,2,1,0:T(8,128)}), f32[1,2,4,3,8,128]{5,4,3,2,1,0:T(8,128)}) %reduce-scatter.2.cloned.1.call-update) | async-done | bytes 98320 | tf_op jit(solution)/shard_map/reduce_scatter | solution.py:187
  146.3 1.1 reshape.46
  147.5 0.2 reshape.47
  147.7 3.4 %reduce-window.6 = f32[16,3,2,2,128]{4,0,2,1,3:T(8,128)S(1)} reduce-window(f32[16,3,2,2,128]{4,0,2,1,3:T(8,128)S(1)} %copy.8, f32[]{:T(128)} %constant.5.clone.1), window={size=1x1x1x1x128 pad=0_0x0_0x0_0x0_0x127_0}, to_apply=%region_1.0 | reduce-window | flops 3121152 | bytes 196612 | tf_op jit(solution)/shard_map/reduce-window
  151.1 0.1 slice.36
  151.2 0.1 copy.9
  151.4 0.1 copy_bitcast_fusion.1
  151.5 0.2 slice_reduce_fusion.2
  151.7 0.7 fusion.1
  152.4 65.8 %pmax.7 = f32[2]{0:T(128)} all-reduce(f32[2]{0:T(128)S(1)} %get-tuple-element.5), channel_id=1, replica_groups=mesh['rows'=32,'feat'=4] {'rows','feat'}, use_global_device_ids=true, to_apply=%region_4.5 | all-reduce | flops 2 | bytes 16 | tf_op jit(solution)/shard_map/pmax | solution.py:203
  (6 shorter events, 0.1 us)
Async XLA Ops:
  7.2 139.2 %reduce-scatter.2.cloned.1.call-start = ((), (), s32[]{:S(2)}) async-start(), calls=%async_computation.1 | async-start | bytes 3244032 | tf_op jit(solution)/shard_map/reduce_scatter | solution.py:187
  7.2 0.7 copy-start
  7.9 0.7 copy-start.1
  8.6 0.7 copy-start.2
  9.3 0.7 copy-start.3
Sparse Core Ops, SparseCore 0:
  64.1 82.1 reduce-scatter.1

commit v2 on v1

--- a/solution.py
+++ b/solution.py
@@ -178,30 +178,222 @@
     )(leaf, live, codes, grad.reshape(blocks, BLOCK), hess.reshape(blocks, BLOCK))
 
 
+MESH = pl.DeviceIdType.MESH
 MIN_CHILD = 20
 ridge_term = 1.0
 
 
+def finish(x):
+    flat = x.reshape(192, 128)
+    row = lax.broadcasted_iota(jnp.int32, (128, 256), 0)
+    col = lax.broadcasted_iota(jnp.int32, (128, 256), 1)
+    same = row // LO == (col % 128) // LO
+    upper = jnp.where(same & ((row <= col) | (col >= 128)), 1.0, 0.0)
+    sums = jnp.dot(flat, upper, precision=lax.Precision.HIGHEST, preferred_element_type=jnp.float32)
+    sub = lax.broadcasted_iota(jnp.int32, (8, 128), 0)
+    gains, tops = [], []
+    for leaf in range(2):
+        top = None
+        for q in range(4):
+            left, total = [], []
+            for s in range(3):
+                at = ((leaf * 4 + q) * 3 + s) * 8
+                inner, whole = sums[at:at + 8, :128], sums[at:at + 8, 128:]
+                run = whole
+                for d in (1, 2, 4):
+                    run = run + jnp.where(sub >= d, pltpu.roll(run, d, 0), 0.0)
+                left.append(inner + (run - whole))
+                total.append(jnp.broadcast_to(run[7:8, :], (8, 128)))
+            right = [t - v for t, v in zip(total, left)]
+            raw = 0.5 * (
+                left[0] ** 2 / (left[1] + ridge_term)
+                + right[0] ** 2 / (right[1] + ridge_term)
+                - total[0] ** 2 / (total[1] + ridge_term)
+            )
+            allowed = (left[2] >= MIN_CHILD) & (right[2] >= MIN_CHILD)
+            gain = jnp.where(allowed, raw, 0.0)
+            gains.append(gain)
+            top = gain if top is None else jnp.maximum(top, gain)
+        tops.append(jnp.broadcast_to(jnp.max(top), (8, 128)))
+    return gains, jnp.where(sub == 0, tops[0], tops[1])
+
+
+def exchange_kernel(hist, gain_ref, best_ref, own, part, hop1, hop2, peak8, peak16,
+                    load_sem, s0, r0, s1, r1, s2, r2, sa, ra, sb, rb):
+    r = lax.axis_index("rows")
+    x = lax.axis_index("feat")
+    c = r % 2
+    z = (r // 2) % 4
+    y = r // 8
+    at = (y, z)
+
+    def rows_id(yy, zz, cc):
+        return {"rows": (yy * 4 + zz) * 2 + cc, "feat": x}
+
+    def along(axis, step):
+        return rows_id((y + step) % 4, z, c) if axis == 0 else rows_id(y, (z + step) % 4, c)
+
+    def octet(d):
+        i = (x * 2 + c + d) % 8
+        return {"rows": (y * 4 + z) * 2 + i % 2, "feat": i // 2}
+
+    def plane(d):
+        return {"rows": ((y * 4 + z + d) % 16) * 2 + c, "feat": x}
+
+    barrier = pltpu.get_barrier_semaphore()
+    for d in range(1, 8):
+        pl.semaphore_signal(barrier, inc=1, device_id=octet(d), device_id_type=MESH)
+    for d in range(1, 16):
+        pl.semaphore_signal(barrier, inc=1, device_id=plane(d), device_id_type=MESH)
+
+    order = (2, 1, 3, 0)
+
+    def source(leaf, k, core):
+        i = (at[leaf] + order[k]) % 4
+        return hist.at[i, :, core, leaf] if leaf == 0 else hist.at[:, i, core, leaf]
+
+    loads = [[pltpu.make_async_copy(source(leaf, k, c), own.at[leaf, k], load_sem.at[leaf, k])
+              for k in range(4)] for leaf in range(2)]
+    for k in range(4):
+        for leaf in range(2):
+            loads[leaf][k].start()
+    pl.semaphore_wait(barrier, 22)
+
+    pairs = [[pltpu.make_async_remote_copy(
+        src_ref=source(leaf, k, 1 - c), dst_ref=part.at[leaf, k],
+        send_sem=s0.at[leaf, k], recv_sem=r0.at[leaf, k],
+        device_id=rows_id(y, z, 1 - c), device_id_type=MESH)
+        for k in range(4)] for leaf in range(2)]
+    for k in range(4):
+        for leaf in range(2):
+            pairs[leaf][k].start()
+
+    def send1(leaf, way, i, k, b):
+        return pltpu.make_async_remote_copy(
+            src_ref=own.at[leaf, k, pl.ds(b, 2)], dst_ref=hop1.at[leaf, way, i],
+            send_sem=s1.at[leaf, way, i], recv_sem=r1.at[leaf, way, i],
+            device_id=along(leaf, 1 if way == 0 else 3), device_id_type=MESH)
+
+    first = [[[send1(leaf, 0, 0, 0, 0), send1(leaf, 0, 1, 1, 2), send1(leaf, 0, 2, 1, 0)],
+              [send1(leaf, 1, 0, 0, 2), send1(leaf, 1, 1, 2, 0), send1(leaf, 1, 2, 2, 2)]] for leaf in range(2)]
+
+    def ready(leaf, k):
+        loads[leaf][k].wait()
+        pairs[leaf][k].wait_recv()
+        own[leaf, k] = own[leaf, k] + part[leaf, k]
+
+    for leaf in range(2):
+        ready(leaf, 0)
+        first[leaf][0][0].start()
+        first[leaf][1][0].start()
+    for leaf in range(2):
+        ready(leaf, 1)
+        first[leaf][0][1].start()
+        ready(leaf, 2)
+        first[leaf][1][1].start()
+    for leaf in range(2):
+        first[leaf][0][0].wait_recv()
+        own[leaf, 1, 0:2] = own[leaf, 1, 0:2] + hop1[leaf, 0, 0]
+        first[leaf][0][2].start()
+        first[leaf][1][0].wait_recv()
+        own[leaf, 2, 2:4] = own[leaf, 2, 2:4] + hop1[leaf, 1, 0]
+        first[leaf][1][2].start()
+    for leaf in range(2):
+        ready(leaf, 3)
+
+    def send2(leaf, way, i, step, row):
+        b = (at[1 - leaf] + step) % 4
+        return pltpu.make_async_remote_copy(
+            src_ref=own.at[leaf, 3, b, pl.ds(row, 48)], dst_ref=hop2.at[leaf, way, i],
+            send_sem=s2.at[leaf, way, i], recv_sem=r2.at[leaf, way, i],
+            device_id=along(1 - leaf, 1 if way == 0 else 3), device_id_type=MESH)
+
+    second = [[[send2(leaf, 0, 0, 2, 0), send2(leaf, 0, 1, 1, 48), send2(leaf, 0, 2, 1, 0)],
+               [send2(leaf, 1, 0, 2, 48), send2(leaf, 1, 1, 3, 0), send2(leaf, 1, 2, 3, 48)]] for leaf in range(2)]
+    for leaf in range(2):
+        for way, i in ((0, 1), (1, 1), (0, 2), (1, 2)):
+            first[leaf][way][i].wait_recv()
+        own[leaf, 3, 0:2] = own[leaf, 3, 0:2] + (hop1[leaf, 0, 2] + hop1[leaf, 1, 1])
+        own[leaf, 3, 2:4] = own[leaf, 3, 2:4] + (hop1[leaf, 0, 1] + hop1[leaf, 1, 2])
+        second[leaf][0][0].start()
+        second[leaf][1][0].start()
+        second[leaf][0][1].start()
+        second[leaf][1][1].start()
+    for leaf in range(2):
+        up, down = (at[1 - leaf] + 1) % 4, (at[1 - leaf] + 3) % 4
+        second[leaf][0][0].wait_recv()
+        own[leaf, 3, up, 0:48] = own[leaf, 3, up, 0:48] + hop2[leaf, 0, 0]
+        second[leaf][0][2].start()
+        second[leaf][1][0].wait_recv()
+        own[leaf, 3, down, 48:96] = own[leaf, 3, down, 48:96] + hop2[leaf, 1, 0]
+        second[leaf][1][2].start()
+    mine = []
+    for leaf in range(2):
+        me = at[1 - leaf]
+        for way, i in ((0, 1), (1, 1), (0, 2), (1, 2)):
+            second[leaf][way][i].wait_recv()
+        mine.append(own[leaf, 3, me, 0:48] + (hop2[leaf, 0, 2] + hop2[leaf, 1, 1]))
+        mine.append(own[leaf, 3, me, 48:96] + (hop2[leaf, 0, 1] + hop2[leaf, 1, 2]))
+
+    gains, top = finish(jnp.concatenate(mine, 0))
+    for i, gain in enumerate(gains):
+        gain_ref[i // 4, i % 4] = gain
+
+    def spread(peaks, n, ssem, rsem, to):
+        copies = [pltpu.make_async_remote_copy(
+            src_ref=peaks.at[0], dst_ref=peaks.at[d], send_sem=ssem.at[d], recv_sem=rsem.at[d],
+            device_id=to(d), device_id_type=MESH) for d in range(1, n)]
+        for copy in copies:
+            copy.start()
+        for copy in copies:
+            copy.wait()
+
+    peak8[0] = top
+    spread(peak8, 8, sa, ra, octet)
+    peak16[0] = jnp.max(peak8[...], 0)
+    spread(peak16, 16, sb, rb, plane)
+    best_ref[...] = jnp.max(peak16[...], 0)
+
+    for leaf in range(2):
+        for k in range(4):
+            pairs[leaf][k].wait_send()
+        for way in range(2):
+            for i in range(3):
+                first[leaf][way][i].wait_send()
+                second[leaf][way][i].wait_send()
+
+
+def exchange(hist):
+    dma = pltpu.SemaphoreType.DMA
+    return pl.pallas_call(
+        exchange_kernel,
+        out_shape=(
+            jax.ShapeDtypeStruct((2, 4, HI, 128), jnp.float32),
+            jax.ShapeDtypeStruct((8, 128), jnp.float32),
+        ),
+        in_specs=[pl.BlockSpec(memory_space=pl.ANY)],
+        out_specs=(pl.BlockSpec(memory_space=pltpu.VMEM), pl.BlockSpec(memory_space=pltpu.VMEM)),
+        scratch_shapes=[
+            pltpu.VMEM((2, 4, 4, 96, 128), jnp.float32),
+            pltpu.VMEM((2, 4, 4, 96, 128), jnp.float32),
+            pltpu.VMEM((2, 2, 3, 2, 96, 128), jnp.float32),
+            pltpu.VMEM((2, 2, 3, 48, 128), jnp.float32),
+            pltpu.VMEM((8, 8, 128), jnp.float32),
+            pltpu.VMEM((16, 8, 128), jnp.float32),
+            dma((2, 4)), dma((2, 4)), dma((2, 4)),
+            dma((2, 2, 3)), dma((2, 2, 3)), dma((2, 2, 3)), dma((2, 2, 3)),
+            dma((8,)), dma((8,)), dma((16,)), dma((16,)),
+        ],
+        name="exchange",
+        compiler_params=pltpu.CompilerParams(collective_id=0, has_side_effects=True, vmem_limit_bytes=16 << 20),
+    )(hist.reshape(4, 4, 2, 2, 96, 128))
+
+
 def local(bin_codes, gradient, hessian, leaf_of_block, block_rows):
     mine = local_hist(bin_codes, gradient, hessian, leaf_of_block, block_rows)
-    mine = lax.psum_scatter(mine, "rows", scatter_dimension=0, tiled=True)
-    histogram = mine.reshape(2, 4, 3, HI, 4, LO).transpose(1, 4, 2, 0, 3, 5).reshape(16, 3, 2, BINS)
-    running = jnp.cumsum(histogram, axis=3)
-    totals = running[..., -1:]
-    left_grad, left_hess, left_count = (running[:, 0], running[:, 1], running[:, 2])
-    total_grad, total_hess, total_count = (totals[:, 0], totals[:, 1], totals[:, 2])
-    right_grad = total_grad - left_grad
-    right_hess = total_hess - left_hess
-    right_count = total_count - left_count
-    raw_gain = 0.5 * (
-        left_grad**2 / (left_hess + ridge_term)
-        + right_grad**2 / (right_hess + ridge_term)
-        - total_grad**2 / (total_hess + ridge_term)
-    )
-    allowed = (left_count >= MIN_CHILD) & (right_count >= MIN_CHILD)
-    split_gain = jnp.transpose(jnp.where(allowed, raw_gain, 0.0), (1, 0, 2))
-    best_gain = lax.pmax(jnp.max(split_gain, axis=(1, 2)), ("rows", "feat"))
-    return (split_gain, best_gain)
+    gain, best = exchange(mine)
+    split_gain = gain.reshape(2, 4, HI, 4, LO).transpose(0, 1, 3, 2, 4).reshape(2, 16, BINS)
+    return split_gain, best[:2, 0]
 
 
 def solution(mesh):

time: 229 us -> 95.5 us (0.42); the launches traced: 225 us -> 96.9 us
  waiting for transfers between devices: 82.3 us -> 0 us
  blocking collectives: 65.8 us -> 0 us
  Pallas kernels: 54.1 us -> 92.1 us
  between operations: 14.1 us -> 0.67 us
  other arithmetic: 4.28 us -> 0 us
    reduce_scatter x1 -> x0, waiting for transfers between devices: 82.3 us -> none  [local(): mine = lax.psum_scatter(mine, 'rows', scatter_dimension=0, tiled=True)]
    pmax x1 -> x0, blocking collectives: 65.8 us -> none  [local(): best_gain = lax.pmax(jnp.max(split_gain, axis=(1, 2)), ('rows', 'feat'))]
    pallas_call x0 -> x1, Pallas kernels: none -> 42 us  [exchange(): pl.pallas_call(exchange_kernel, out_shape=(jax.ShapeDtypeStruct((2, 4, HI...]
    pallas_call x1, Pallas kernels: 54.1 us -> 50.1 us  [local_hist(): pl.pallas_call(hist_kernel, out_shape=jax.ShapeDtypeStruct((feats // 16,...]
    another operation x3 -> x0, other arithmetic: 3.56 us -> none
  transfers between devices with their start and end apart: 1 -> 0, of which waited for: 1 -> 0; matrix products, arithmetic and copies ran while one was open for 0% -> 0% of each run, Pallas kernels for 0% -> 0%
where the time goes in v2:
time: 95.5 us; the launch traced here: 96.9 us
  Pallas kernels  92.1 us (96%)
  local copies, waits for them, and re-layouts  4.16 us (4%)
    pallas_call x1, Pallas kernels, local_hist(): pl.pallas_call(hist_kernel, out_shape=jax.ShapeDtypeStruct((feats // 16,...  50.1 us
    pallas_call x1, Pallas kernels, exchange(): pl.pallas_call(exchange_kernel, out_shape=(jax.ShapeDtypeStruct((2, 4, HI...  42 us
    unnamed x8, local copies, waits for them, and re-layouts  2.7 us

profile of v2, /device:TPU:1, one launch (start us, length us, event | category | flops | bytes accessed | tf_op | source)
XLA Modules:
  0.0 96.9 jit_solution(17782673290315069077)
XLA Ops:
  0.6 0.0 copy-start
  0.6 0.7 copy-done
  1.3 0.0 copy-start.1
  1.3 0.7 copy-done.1
  2.0 0.0 copy-start.2
  2.0 0.7 copy-done.2
  2.7 0.0 copy-start.3
  2.7 0.7 copy-done.3
  3.3 50.1 %histogram.1 = f32[32,2,4,3,8,128]{5,4,3,2,1,0:T(8,128)S(1)} custom-call(s32[32]{0:T(128)S(1)} %copy-done.2, s32[32]{0:T(128)S(1)} %copy-done.3, s32[4096,512]{1,0:T(8,128)} %codes_ref.1, bf16[32,128]{1,0:T(8,128)(2,1)S(1)} %bitcast.9, bf16[32,128]{1,0:T(8,128)(2,1)S(1)} %bitcast.10), custom_call_target="tpu_custom_call" | custom-call | tf_op jit(solution)/shard_map/histogram/pallas_call | solution.py:172
  53.4 42.0 %exchange.1 = (f32[2,4,8,128]{3,2,1,0:T(8,128)S(1)}, f32[8,128]{1,0:T(8,128)S(1)}) custom-call(f32[4,4,2,2,96,128]{5,4,3,2,1,0:T(8,128)S(1)} %bitcast.8), custom_call_target="tpu_custom_call" | custom-call | tf_op jit(solution)/shard_map/exchange/pallas_call | solution.py:368
  95.4 0.6 slice_reduce_fusion
  96.1 0.1 reshape.22
  96.2 0.7 reshape.23
  (1 shorter events, 0.0 us)
Async XLA Ops:
  0.6 0.7 copy-start
  1.3 0.7 copy-start.1
  2.0 0.7 copy-start.2
  2.7 0.7 copy-start.3

commit v3 on v2

--- a/solution.py
+++ b/solution.py
@@ -1,4 +1,3 @@
-import functools
 import jax
 import jax.numpy as jnp
 from jax import lax
@@ -13,168 +12,201 @@
 HI = 8
 FSTEP = 128
 GROUP = 8
-
-
-def hist_kernel(leaf_ref, live_ref, codes_ref, grad_ref, hess_ref, out_ref,
-                compact, lo_ref, hi_ref, pair_ref, ones_ref, stat_ref, gf, hf):
+GROUPS = 8
+TILE = 256
+
+
+def hist_kernel(leaf_hbm, live_hbm, codes_hbm, grad_hbm, hess_hbm, out_hbm,
+                leaf_ref, live_ref, table, codes_ref, grad_ref, hess_ref, lo_ref, hi_ref,
+                g_ref, h_ref, c_ref, stat_ref, gf, hf, out_ref, small_sem, code_sem, out_sem):
     blocks = leaf_ref.shape[0]
-    tiles = lo_ref.shape[0]
-    first = pl.program_id(0) == 0
-
-    def count(k, c):
-        n = (live_ref[k] + 7) // 8 * 8
-        one = leaf_ref[k]
-        return c[0] + n * (1 - one), c[1] + n * one
-
-    rows0, rows1 = lax.fori_loop(0, blocks, count, (jnp.int32(0), jnp.int32(0)))
-    tiles0 = (rows0 + 255) // 256
-    tiles1 = (rows1 + 255) // 256
-    base1 = tiles0 * 256
-
-    @pl.when(first)
-    def _():
-        gf[...] = grad_ref[...].astype(jnp.float32)
-        hf[...] = hess_ref[...].astype(jnp.float32)
-        stat_ref[...] = jnp.zeros_like(stat_ref)
-        lane = lax.broadcasted_iota(jnp.int32, (8, 128), 1)
-        sub = lax.broadcasted_iota(jnp.int32, (8, 128), 0)
-
-        def place(k, off):
+    steps = codes_ref.shape[0]
+    per_table = table.shape[0] // 2
+    bf16 = jnp.bfloat16
+
+    small = [pltpu.make_async_copy(a, b, small_sem.at[i]) for i, (a, b) in enumerate(
+        ((leaf_hbm, leaf_ref), (live_hbm, live_ref), (grad_hbm, grad_ref), (hess_hbm, hess_ref)))]
+    for copy in small:
+        copy.start()
+
+    def codes_copy(i):
+        return pltpu.make_async_copy(
+            codes_hbm.at[:, pl.ds(pl.multiple_of(i * FSTEP, FSTEP), FSTEP)], codes_ref.at[i], code_sem.at[i])
+
+    codes_copy(0).start()
+    stat_ref[...] = jnp.zeros_like(stat_ref)
+    for copy in small:
+        copy.wait()
+    gf[...] = grad_ref[...].astype(jnp.float32)
+    hf[...] = hess_ref[...].astype(jnp.float32)
+    lane = lax.broadcasted_iota(jnp.int32, (8, 128), 1)
+    sub = lax.broadcasted_iota(jnp.int32, (8, 128), 0)
+
+    def place(k4, c):
+        off0, off1 = c
+        for d in range(4):
+            k = k4 * 4 + d
             n = live_ref[k]
+            leaf = leaf_ref[k]
+            off = jnp.where(leaf == 0, off0, off1)
+            for i in range(BLOCK // 8):
+                table[leaf * per_table + off + i] = k * BLOCK + 8 * i
             g = jnp.broadcast_to(gf[pl.ds(k, 1), :], (8, 128))
             h = jnp.broadcast_to(hf[pl.ds(k, 1), :], (8, 128))
             s = jnp.where(sub == 0, g, jnp.where(sub == 1, h, jnp.where(sub == 2, 1.0, 0.0)))
             s = jnp.where(lane < n, s, 0.0)
-            shift = off % 128
+            shift = off * 8 % 128
             rolled = pltpu.roll(s, shift, 1)
-            at = off // 128
-            stat_ref[at] += jnp.where(lane >= shift, rolled, 0.0)
-            stat_ref[at + 1] += jnp.where(lane < shift, rolled, 0.0)
-            return off + (n + 7) // 8 * 8
-
-        def pick(leaf, k, off):
-            return lax.cond(leaf_ref[k] == leaf, lambda: place(k, off), lambda: off)
-
-        lax.fori_loop(0, blocks, functools.partial(pick, 0), jnp.int32(0))
-        lax.fori_loop(0, blocks, functools.partial(pick, 1), base1)
-
-        @pl.loop(0, tiles)
+            at = off * 8 // 128
+            stat_ref[leaf, at] += jnp.where(lane >= shift, rolled, 0.0)
+            stat_ref[leaf, at + 1] += jnp.where(lane < shift, rolled, 0.0)
+            off = off + (n + 7) // 8
+            off0 = jnp.where(leaf == 0, off, off0)
+            off1 = jnp.where(leaf == 0, off1, off)
+        return off0, off1
+
+    ends = lax.fori_loop(0, blocks // 4, place, (jnp.int32(0), jnp.int32(0)))
+    tiles = [(end * 8 + TILE - 1) // TILE for end in ends]
+    for leaf in range(2):
+        for i in range(TILE // 8):
+            table[leaf * per_table + ends[leaf] + i] = 0
+
+        @pl.loop(0, tiles[leaf])
         def _(t):
             for half in range(2):
-                s = stat_ref[2 * t + half]
-                g, h, c = (jnp.broadcast_to(s[i:i + 1, :], (8, 128)) for i in range(3))
-                pair_ref[t, :, half * 128:half * 128 + 128] = jnp.concatenate([g, h], 0).astype(jnp.bfloat16)
-                ones_ref[t, :, half * 128:half * 128 + 128] = jnp.concatenate([c, c], 0).astype(jnp.bfloat16)
-
-    def move(leaf, k, off):
-        def go():
-            at = pl.multiple_of(off, 8)
-            compact[pl.ds(at, BLOCK), :] = codes_ref[pl.ds(pl.multiple_of(k * BLOCK, BLOCK), BLOCK), :]
-            return off + (live_ref[k] + 7) // 8 * 8
-        return lax.cond(leaf_ref[k] == leaf, go, lambda: off)
-
-    lax.fori_loop(0, blocks, functools.partial(move, 0), jnp.int32(0))
-    lax.fori_loop(0, blocks, functools.partial(move, 1), base1)
-
-    @pl.loop(0, (tiles0 + tiles1 + 1) // 2)
-    def _(u):
-        at = pl.multiple_of(u * 512, 512)
-        word = compact[pl.ds(at, 128), :] & 255
-        for q in range(1, 4):
-            word = word | ((compact[pl.ds(at + 128 * q, 128), :] & 255) << (8 * q))
-        word = word.T
-        for q in range(4):
-            lo = (word >> (8 * q)) & (LO - 1)
-            hi = (word >> (8 * q + 5)) & (HI - 1)
-            lanes = slice(128 * (q % 2), 128 * (q % 2) + 128)
-            lo_ref[2 * u + q // 2, :, lanes] = lo.astype(jnp.float32)
-            hi_ref[2 * u + q // 2, :, lanes] = hi.astype(jnp.float32)
-
-    sub16 = lax.broadcasted_iota(jnp.int32, (16, 256), 0)
-    lo_a = sub16.astype(jnp.float32).astype(jnp.bfloat16)
-    lo_b = (sub16 + 16).astype(jnp.float32).astype(jnp.bfloat16)
-    hi_n = (sub16 % 8).astype(jnp.float32).astype(jnp.bfloat16)
-    one = jnp.ones((16, 256), jnp.bfloat16)
-    zero = jnp.zeros((16, 256), jnp.bfloat16)
-    lane_group = lax.broadcasted_iota(jnp.int32, (8, 128), 1) // LO
-
-    groups = 8
-    for leaf in range(2):
-        for part in range(FSTEP // (groups * GROUP)):
-            def run(*accs, leaf=leaf, part=part):
-                def step(t, carry):
-                    pair = pair_ref[t]
-                    ones = ones_ref[t]
-                    for i in range(groups):
-                        rhs, lhs = [], []
-                        for f2 in range(0, GROUP, 2):
-                            his = []
-                            for d in range(2):
-                                f = part * groups * GROUP + i * GROUP + f2 + d
-                                low = jnp.broadcast_to(lo_ref[t, f:f + 1, :], (16, 256)).astype(jnp.bfloat16)
-                                rhs.append(jnp.where(low == lo_a, one, zero))
-                                rhs.append(jnp.where(low == lo_b, one, zero))
-                                high = jnp.broadcast_to(hi_ref[t, f:f + 1, :], (8, 256))
-                                his.append(high)
-                                high = jnp.concatenate([high, high], 0).astype(jnp.bfloat16)
-                                lhs.append(jnp.where(high == hi_n, pair, zero))
-                            both = jnp.concatenate(his, 0).astype(jnp.bfloat16)
-                            lhs.append(jnp.where(both == hi_n, ones, zero))
-                        stage = (i // 2) % 2
-                        pltpu.matmul_push_rhs(jnp.concatenate(rhs, 0), stage, i % 2, transpose=True)
-                        pltpu.matmul_acc_lhs(accs[i], jnp.concatenate(lhs, 0), load_staged_rhs=stage)
-                    return carry
-
-                lo_t = 0 if leaf == 0 else tiles0
-                hi_t = tiles0 if leaf == 0 else tiles0 + tiles1
-                lax.fori_loop(lo_t, hi_t, step, 0)
-                for i in range(groups):
-                    sums = pltpu.matmul_pop(accs[i])
-                    for q in range(2):
-                        for s in range(3):
-                            tile = None
-                            for d in range(4):
-                                f = 4 * q + d
-                                row = 48 * (f // 2) + (16 * (f % 2) + 8 * s if s < 2 else 32 + 8 * (f % 2))
-                                piece = sums[row:row + 8, 128 * q:128 * q + 128]
-                                tile = piece if tile is None else jnp.where(lane_group == d, piece, tile)
-                            gq = (part * groups + i) * 2 + q
-                            out_ref[gq // 4, leaf, gq % 4, s] = tile
-
-            pl.run_scoped(run, *[AccMemorySpace(i % 2)((24 * GROUP, 256), jnp.float32) for i in range(groups)])
+                s = stat_ref[leaf, 2 * t + half]
+                for i, ref in enumerate((g_ref, h_ref, c_ref)):
+                    ref[leaf, t, :, half * 128:half * 128 + 128] = jnp.broadcast_to(s[i:i + 1, :], (16, 128)).astype(bf16)
+
+    sub8 = lax.broadcasted_iota(jnp.int32, (16, TILE), 0) % 8
+    lo_n = [(sub8 + 8 * k).astype(jnp.float32).astype(bf16) for k in range(4)]
+    hi_n = lo_n[0]
+    one = jnp.ones((16, TILE), bf16)
+    zero = jnp.zeros((16, TILE), bf16)
+    which = 2 * (lane // 64) + lane // 8 % 2
+
+    def turn(step, leaf, t, half):
+        at = leaf * per_table + t * (TILE // 8) + half * (BLOCK // 8)
+        rows = [codes_ref[step, pl.ds(pl.multiple_of(table[at + i], 8), 8), :] for i in range(BLOCK // 8)]
+        word = jnp.concatenate(rows, 0).T
+        lanes = slice(BLOCK * half, BLOCK * half + BLOCK)
+        to = (0 if leaf == 0 else tiles[0]) + t
+        lo_ref[step % 2, to, :, lanes] = (word & (LO - 1)).astype(jnp.float32)
+        hi_ref[step % 2, to, :, lanes] = (word >> 5).astype(jnp.float32)
+
+    codes_copy(0).wait()
+    for i in range(1, steps):
+        codes_copy(i).start()
+    for leaf in range(2):
+        @pl.loop(0, tiles[leaf])
+        def _(t):
+            for half in range(2):
+                turn(0, leaf, t, half)
+
+    @pl.loop(0, steps)
+    def _(step):
+        slot = step % 2
+        later = jnp.minimum(step + 1, steps - 1)
+
+        @pl.when(step + 1 < steps)
+        def _():
+            codes_copy(later).wait()
+
+        for leaf in range(2):
+            base = 0 if leaf == 0 else tiles[0]
+            for half in range(FSTEP // (GROUPS * GROUP)):
+                def run(*accs, leaf=leaf, half=half, base=base):
+                    def pair(ref, t, i, p):
+                        f = (half * GROUPS + i) * GROUP + 2 * p
+                        return jnp.concatenate([jnp.broadcast_to(ref[slot, base + t, f + d:f + d + 1, :], (8, TILE))
+                                                for d in range(2)], 0).astype(bf16)
+
+                    def push(t, i):
+                        rhs = []
+                        for p in range(GROUP // 2):
+                            low = pair(lo_ref, t, i, p)
+                            rhs += [jnp.where(low == n, one, zero) for n in lo_n]
+                        hot = jnp.concatenate(rhs, 0).astype(jnp.float8_e4m3fn)
+                        pltpu.matmul_push_rhs(hot, (i // 2) % 2, i % 2, transpose=True)
+
+                    def tile_step(t, carry):
+                        stats = [ref[leaf, t] for ref in (g_ref, h_ref, c_ref)]
+                        for i in range(GROUPS):
+                            if i >= 2:
+                                push(t, i)
+                            lhs = []
+                            for p in range(GROUP // 2):
+                                hit = pair(hi_ref, t, i, p) == hi_n
+                                lhs += [jnp.where(hit, s, zero) for s in stats]
+                            pltpu.matmul_acc_lhs(accs[i], jnp.concatenate(lhs, 0), load_staged_rhs=(i // 2) % 2)
+                        for i in range(2):
+                            push(t + 1, i)
+                        turn(later, leaf, t, half)
+                        return carry
+
+                    for i in range(2):
+                        push(0, i)
+                    lax.fori_loop(0, tiles[leaf], tile_step, 0)
+                    for i in range(2):
+                        pltpu.matmul_acc_lhs(accs[GROUPS + i], zero, load_staged_rhs=0)
+                    for i in range(GROUPS):
+                        sums = pltpu.matmul_pop(accs[i])
+                        for q in range(2):
+                            for s in range(3):
+                                tile = None
+                                for d in range(4):
+                                    row = 48 * (2 * q + d // 2) + 16 * s + 8 * (d % 2)
+                                    piece = sums[row:row + 8, 128 * q:128 * q + 128]
+                                    tile = piece if tile is None else jnp.where(which == d, piece, tile)
+                                gq = (half * GROUPS + i) * 2 + q
+                                out_ref[step * (FSTEP // 16) + gq // 4, leaf, gq % 4, s] = tile
+
+                pl.run_scoped(run, *[AccMemorySpace(i % 2)((24 * GROUP, 256), jnp.float32) for i in range(GROUPS)],
+                              *[AccMemorySpace(i)((16, 256), jnp.float32) for i in range(2)])
+        out_copy(out_ref, out_hbm, out_sem, step).start()
+
+    for i in range(steps):
+        out_copy(out_ref, out_hbm, out_sem, i).wait()
+
+
+def out_copy(out_ref, out_hbm, out_sem, i):
+    part = pl.ds(i * (FSTEP // 16), FSTEP // 16)
+    return pltpu.make_async_copy(out_ref.at[part], out_hbm.at[part], out_sem.at[i])
 
 
 def local_hist(codes, grad, hess, leaf, live):
     rows, feats = codes.shape
     blocks = leaf.shape[0]
-    tiles = rows // 256 + 2
-    owners = FSTEP // 16
-    spec = pltpu.PrefetchScalarGridSpec(
-        num_scalar_prefetch=2,
-        grid=(feats // FSTEP,),
-        in_specs=[
-            pl.BlockSpec((rows, FSTEP), lambda i, *_: (0, i)),
-            pl.BlockSpec((blocks, BLOCK), lambda i, *_: (0, 0)),
-            pl.BlockSpec((blocks, BLOCK), lambda i, *_: (0, 0)),
-        ],
-        out_specs=pl.BlockSpec((owners, 2, 4, 3, 8, 128), lambda i, *_: (i, 0, 0, 0, 0, 0)),
+    tiles = rows // TILE
+    steps = feats // FSTEP
+    hbm = pl.BlockSpec(memory_space=pltpu.HBM)
+    out = (feats // 16, 2, 4, 3, 8, 128)
+    dma = pltpu.SemaphoreType.DMA
+    return pl.pallas_call(
+        hist_kernel,
+        out_shape=jax.ShapeDtypeStruct(out, jnp.float32),
+        in_specs=[hbm] * 5,
+        out_specs=hbm,
         scratch_shapes=[
-            pltpu.VMEM((tiles * 256 + BLOCK, FSTEP), jnp.int32),
-            pltpu.VMEM((tiles, FSTEP, 256), jnp.float32),
-            pltpu.VMEM((tiles, FSTEP, 256), jnp.float32),
-            pltpu.VMEM((tiles, 16, 256), jnp.bfloat16),
-            pltpu.VMEM((tiles, 16, 256), jnp.bfloat16),
-            pltpu.VMEM((2 * tiles + 1, 8, 128), jnp.float32),
+            pltpu.SMEM((blocks,), jnp.int32),
+            pltpu.SMEM((blocks,), jnp.int32),
+            pltpu.SMEM((2 * (rows // 8 + TILE // 8 + 16),), jnp.int32),
+            pltpu.VMEM((steps, rows, FSTEP), jnp.int32),
+            pltpu.VMEM((blocks, BLOCK), jnp.bfloat16),
+            pltpu.VMEM((blocks, BLOCK), jnp.bfloat16),
+            pltpu.VMEM((2, tiles + 2, FSTEP, TILE), jnp.float32),
+            pltpu.VMEM((2, tiles + 2, FSTEP, TILE), jnp.float32),
+            pltpu.VMEM((2, tiles, 16, TILE), jnp.bfloat16),
+            pltpu.VMEM((2, tiles, 16, TILE), jnp.bfloat16),
+            pltpu.VMEM((2, tiles, 16, TILE), jnp.bfloat16),
+            pltpu.VMEM((2, 2 * tiles + 2, 8, 128), jnp.float32),
             pltpu.VMEM((blocks, BLOCK), jnp.float32),
             pltpu.VMEM((blocks, BLOCK), jnp.float32),
+            pltpu.VMEM(out, jnp.float32),
+            dma((4,)), dma((steps,)), dma((steps,)),
         ],
-    )
-    return pl.pallas_call(
-        hist_kernel,
-        out_shape=jax.ShapeDtypeStruct((feats // 16, 2, 4, 3, 8, 128), jnp.float32),
-        grid_spec=spec,
         name="histogram",
-        compiler_params=pltpu.CompilerParams(vmem_limit_bytes=48 << 20),
+        compiler_params=pltpu.CompilerParams(vmem_limit_bytes=67043328),
     )(leaf, live, codes, grad.reshape(blocks, BLOCK), hess.reshape(blocks, BLOCK))
 
 
@@ -187,8 +219,9 @@
     flat = x.reshape(192, 128)
     row = lax.broadcasted_iota(jnp.int32, (128, 256), 0)
     col = lax.broadcasted_iota(jnp.int32, (128, 256), 1)
-    same = row // LO == (col % 128) // LO
-    upper = jnp.where(same & ((row <= col) | (col >= 128)), 1.0, 0.0)
+    same = 2 * (row // 64) + row // 8 % 2 == (col % 128) // LO
+    upto = 8 * (row // 16 % 4) + row % 8 <= col % LO
+    upper = jnp.where(same & (upto | (col >= 128)), 1.0, 0.0)
     sums = jnp.dot(flat, upper, precision=lax.Precision.HIGHEST, preferred_element_type=jnp.float32)
     sub = lax.broadcasted_iota(jnp.int32, (8, 128), 0)
     gains, tops = [], []
@@ -385,7 +418,7 @@
             dma((8,)), dma((8,)), dma((16,)), dma((16,)),
         ],
         name="exchange",
-        compiler_params=pltpu.CompilerParams(collective_id=0, has_side_effects=True, vmem_limit_bytes=16 << 20),
+        compiler_params=pltpu.CompilerParams(collective_id=0, has_side_effects=True, vmem_limit_bytes=67043328),
     )(hist.reshape(4, 4, 2, 2, 96, 128))
 
 

time: 95.5 us -> 67.4 us (0.71); the launches traced: 96.9 us -> 67.9 us
  Pallas kernels: 92.1 us -> 64.3 us
  local copies, waits for them, and re-layouts: 4.16 us -> 2.9 us
    pallas_call x1, Pallas kernels: 50.1 us -> 26.9 us  [local_hist(): pl.pallas_call(hist_kernel, out_shape=jax.ShapeDtypeStruct(out, jnp.float...]
    pallas_call x1, Pallas kernels: 42 us -> 37.3 us  [exchange(): pl.pallas_call(exchange_kernel, out_shape=(jax.ShapeDtypeStruct((2, 4, HI...]
    unnamed x8 -> x0, local copies, waits for them, and re-layouts: 2.7 us -> none
where the time goes in v3:
time: 67.4 us; the launch traced here: 67.9 us
  Pallas kernels  64.3 us (95%)
  local copies, waits for them, and re-layouts  2.9 us (4%)
    pallas_call x1, Pallas kernels, exchange(): pl.pallas_call(exchange_kernel, out_shape=(jax.ShapeDtypeStruct((2, 4, HI...  37.3 us
    pallas_call x1, Pallas kernels, local_hist(): pl.pallas_call(hist_kernel, out_shape=jax.ShapeDtypeStruct(out, jnp.float...  26.9 us
    reshape x2, local copies, waits for them, and re-layouts, local(): gain.reshape(2, 4, HI, 4, LO).transpose(0, 1, 3, 2, 4).reshape(2, 16, BINS)  1.58 us

profile of v3, /device:TPU:1, one launch (start us, length us, event | category | flops | bytes accessed | tf_op | source)
XLA Modules:
  0.0 67.9 jit_solution(3881135344417599839)
XLA Ops:
  0.6 26.9 %histogram.1 = f32[32,2,4,3,8,128]{5,4,3,2,1,0:T(8,128)} custom-call(s32[32]{0:T(128)} %leaf_hbm.1, s32[32]{0:T(128)} %live_hbm.1, s32[4096,512]{1,0:T(8,128)} %codes_hbm.1, bf16[32,128]{1,0:T(8,128)(2,1)} %bitcast.10, bf16[32,128]{1,0:T(8,128)(2,1)} %bitcast.11), custom_call_target="tpu_custom_call" | custom-call | tf_op jit(solution)/shard_map/histogram/pallas_call | solution.py:185
  27.6 37.3 %exchange.1 = (f32[2,4,8,128]{3,2,1,0:T(8,128)}, f32[8,128]{1,0:T(8,128)}) custom-call(f32[4,4,2,2,96,128]{5,4,3,2,1,0:T(8,128)} %bitcast.8), custom_call_target="tpu_custom_call" | custom-call | tf_op jit(solution)/shard_map/exchange/pallas_call | solution.py:401
  64.9 1.3 %slice_reduce_fusion = f32[2]{0:T(128)} fusion(f32[8,128]{1,0:T(8,128)} %get-tuple-element.5), kind=kLoop, calls=%fused_computation | loop fusion | bytes 16 | tf_op jit(solution)/shard_map/slice | solution.py:429
  66.3 0.9 %reshape.22 = f32[2,4,8,4,32]{4,3,2,1,0:T(4,128)S(1)} reshape(f32[2,4,8,128]{3,2,1,0:T(8,128)} %get-tuple-element.4) | data formatting | bytes 65536 | tf_op jit(solution)/shard_map/reshape | solution.py:428
  67.1 0.7 %reshape.23 = f32[2,16,256]{2,1,0:T(8,128)} reshape(f32[2,4,4,8,32]{4,3,2,1,0:T(8,128)S(1)} %copy.8) | data formatting | bytes 65536 | tf_op jit(solution)/shard_map/reshape | solution.py:428
  (1 shorter events, 0.0 us)

commit v4 on v3

--- a/solution.py
+++ b/solution.py
@@ -49,17 +49,19 @@
             n = live_ref[k]
             leaf = leaf_ref[k]
             off = jnp.where(leaf == 0, off0, off1)
+            to = leaf * per_table + off
+            shift = k * BLOCK - 8 * off
             for i in range(BLOCK // 8):
-                table[leaf * per_table + off + i] = k * BLOCK + 8 * i
+                table[to + i] = shift
             g = jnp.broadcast_to(gf[pl.ds(k, 1), :], (8, 128))
             h = jnp.broadcast_to(hf[pl.ds(k, 1), :], (8, 128))
             s = jnp.where(sub == 0, g, jnp.where(sub == 1, h, jnp.where(sub == 2, 1.0, 0.0)))
             s = jnp.where(lane < n, s, 0.0)
-            shift = off * 8 % 128
-            rolled = pltpu.roll(s, shift, 1)
-            at = off * 8 // 128
-            stat_ref[leaf, at] += jnp.where(lane >= shift, rolled, 0.0)
-            stat_ref[leaf, at + 1] += jnp.where(lane < shift, rolled, 0.0)
+            turned = lax.rem(off, 16) * 8
+            rolled = pltpu.roll(s, turned, 1)
+            at = off // 16
+            stat_ref[leaf, at] += jnp.where(lane >= turned, rolled, 0.0)
+            stat_ref[leaf, at + 1] += jnp.where(lane < turned, rolled, 0.0)
             off = off + (n + 7) // 8
             off0 = jnp.where(leaf == 0, off, off0)
             off1 = jnp.where(leaf == 0, off1, off)
@@ -69,7 +71,7 @@
     tiles = [(end * 8 + TILE - 1) // TILE for end in ends]
     for leaf in range(2):
         for i in range(TILE // 8):
-            table[leaf * per_table + ends[leaf] + i] = 0
+            table[leaf * per_table + ends[leaf] + i] = -8 * ends[leaf]
 
         @pl.loop(0, tiles[leaf])
         def _(t):
@@ -86,8 +88,9 @@
     which = 2 * (lane // 64) + lane // 8 % 2
 
     def turn(step, leaf, t, half):
-        at = leaf * per_table + t * (TILE // 8) + half * (BLOCK // 8)
-        rows = [codes_ref[step, pl.ds(pl.multiple_of(table[at + i], 8), 8), :] for i in range(BLOCK // 8)]
+        first = t * (TILE // 8) + half * (BLOCK // 8)
+        rows = [codes_ref[step, pl.ds(pl.multiple_of(table[leaf * per_table + first + i] + 8 * (first + i), 8), 8), :]
+                for i in range(BLOCK // 8)]
         word = jnp.concatenate(rows, 0).T
         lanes = slice(BLOCK * half, BLOCK * half + BLOCK)
         to = (0 if leaf == 0 else tiles[0]) + t
@@ -247,8 +250,8 @@
             gain = jnp.where(allowed, raw, 0.0)
             gains.append(gain)
             top = gain if top is None else jnp.maximum(top, gain)
-        tops.append(jnp.broadcast_to(jnp.max(top), (8, 128)))
-    return gains, jnp.where(sub == 0, tops[0], tops[1])
+        tops.append(jnp.broadcast_to(jnp.max(top), (2, 128)))
+    return gains, jnp.where(sub[:2] == 0, tops[0], tops[1])
 
 
 def exchange_kernel(hist, gain_ref, best_ref, own, part, hop1, hop2, peak8, peak16,
@@ -276,8 +279,9 @@
     barrier = pltpu.get_barrier_semaphore()
     for d in range(1, 8):
         pl.semaphore_signal(barrier, inc=1, device_id=octet(d), device_id_type=MESH)
-    for d in range(1, 16):
-        pl.semaphore_signal(barrier, inc=1, device_id=plane(d), device_id_type=MESH)
+    for axis in range(2):
+        for step in (1, 2, 3):
+            pl.semaphore_signal(barrier, inc=1, device_id=along(axis, step), device_id_type=MESH)
 
     order = (2, 1, 3, 0)
 
@@ -290,7 +294,7 @@
     for k in range(4):
         for leaf in range(2):
             loads[leaf][k].start()
-    pl.semaphore_wait(barrier, 22)
+    pl.semaphore_wait(barrier, 13)
 
     pairs = [[pltpu.make_async_remote_copy(
         src_ref=source(leaf, k, 1 - c), dst_ref=part.at[leaf, k],
@@ -334,39 +338,25 @@
     for leaf in range(2):
         ready(leaf, 3)
 
-    def send2(leaf, way, i, step, row):
-        b = (at[1 - leaf] + step) % 4
+    def send2(leaf, step):
         return pltpu.make_async_remote_copy(
-            src_ref=own.at[leaf, 3, b, pl.ds(row, 48)], dst_ref=hop2.at[leaf, way, i],
-            send_sem=s2.at[leaf, way, i], recv_sem=r2.at[leaf, way, i],
-            device_id=along(1 - leaf, 1 if way == 0 else 3), device_id_type=MESH)
-
-    second = [[[send2(leaf, 0, 0, 2, 0), send2(leaf, 0, 1, 1, 48), send2(leaf, 0, 2, 1, 0)],
-               [send2(leaf, 1, 0, 2, 48), send2(leaf, 1, 1, 3, 0), send2(leaf, 1, 2, 3, 48)]] for leaf in range(2)]
+            src_ref=own.at[leaf, 3, (at[1 - leaf] + step) % 4], dst_ref=hop2.at[leaf, step - 1],
+            send_sem=s2.at[leaf, step - 1], recv_sem=r2.at[leaf, step - 1],
+            device_id=along(1 - leaf, step), device_id_type=MESH)
+
+    second = [[send2(leaf, step) for step in (2, 1, 3)] for leaf in range(2)]
     for leaf in range(2):
         for way, i in ((0, 1), (1, 1), (0, 2), (1, 2)):
             first[leaf][way][i].wait_recv()
         own[leaf, 3, 0:2] = own[leaf, 3, 0:2] + (hop1[leaf, 0, 2] + hop1[leaf, 1, 1])
         own[leaf, 3, 2:4] = own[leaf, 3, 2:4] + (hop1[leaf, 0, 1] + hop1[leaf, 1, 2])
-        second[leaf][0][0].start()
-        second[leaf][1][0].start()
-        second[leaf][0][1].start()
-        second[leaf][1][1].start()
-    for leaf in range(2):
-        up, down = (at[1 - leaf] + 1) % 4, (at[1 - leaf] + 3) % 4
-        second[leaf][0][0].wait_recv()
-        own[leaf, 3, up, 0:48] = own[leaf, 3, up, 0:48] + hop2[leaf, 0, 0]
-        second[leaf][0][2].start()
-        second[leaf][1][0].wait_recv()
-        own[leaf, 3, down, 48:96] = own[leaf, 3, down, 48:96] + hop2[leaf, 1, 0]
-        second[leaf][1][2].start()
+        for copy in second[leaf]:
+            copy.start()
     mine = []
     for leaf in range(2):
-        me = at[1 - leaf]
-        for way, i in ((0, 1), (1, 1), (0, 2), (1, 2)):
-            second[leaf][way][i].wait_recv()
-        mine.append(own[leaf, 3, me, 0:48] + (hop2[leaf, 0, 2] + hop2[leaf, 1, 1]))
-        mine.append(own[leaf, 3, me, 48:96] + (hop2[leaf, 0, 1] + hop2[leaf, 1, 2]))
+        for copy in second[leaf]:
+            copy.wait_recv()
+        mine.append((own[leaf, 3, at[1 - leaf]] + hop2[leaf, 0]) + (hop2[leaf, 1] + hop2[leaf, 2]))
 
     gains, top = finish(jnp.concatenate(mine, 0))
     for i, gain in enumerate(gains):
@@ -381,11 +371,11 @@
         for copy in copies:
             copy.wait()
 
-    peak8[0] = top
+    peak16[0] = top
+    spread(peak16, 16, sb, rb, plane)
+    peak8[0] = jnp.max(peak16[...], 0)
     spread(peak8, 8, sa, ra, octet)
-    peak16[0] = jnp.max(peak8[...], 0)
-    spread(peak16, 16, sb, rb, plane)
-    best_ref[...] = jnp.max(peak16[...], 0)
+    best_ref[...] = jnp.max(peak8[...], 0)
 
     for leaf in range(2):
         for k in range(4):
@@ -393,7 +383,8 @@
         for way in range(2):
             for i in range(3):
                 first[leaf][way][i].wait_send()
-                second[leaf][way][i].wait_send()
+        for copy in second[leaf]:
+            copy.wait_send()
 
 
 def exchange(hist):
@@ -402,7 +393,7 @@
         exchange_kernel,
         out_shape=(
             jax.ShapeDtypeStruct((2, 4, HI, 128), jnp.float32),
-            jax.ShapeDtypeStruct((8, 128), jnp.float32),
+            jax.ShapeDtypeStruct((2, 128), jnp.float32),
         ),
         in_specs=[pl.BlockSpec(memory_space=pl.ANY)],
         out_specs=(pl.BlockSpec(memory_space=pltpu.VMEM), pl.BlockSpec(memory_space=pltpu.VMEM)),
@@ -410,15 +401,15 @@
             pltpu.VMEM((2, 4, 4, 96, 128), jnp.float32),
             pltpu.VMEM((2, 4, 4, 96, 128), jnp.float32),
             pltpu.VMEM((2, 2, 3, 2, 96, 128), jnp.float32),
-            pltpu.VMEM((2, 2, 3, 48, 128), jnp.float32),
-            pltpu.VMEM((8, 8, 128), jnp.float32),
-            pltpu.VMEM((16, 8, 128), jnp.float32),
+            pltpu.VMEM((2, 3, 96, 128), jnp.float32),
+            pltpu.VMEM((8, 2, 128), jnp.float32),
+            pltpu.VMEM((16, 2, 128), jnp.float32),
             dma((2, 4)), dma((2, 4)), dma((2, 4)),
-            dma((2, 2, 3)), dma((2, 2, 3)), dma((2, 2, 3)), dma((2, 2, 3)),
+            dma((2, 2, 3)), dma((2, 2, 3)), dma((2, 3)), dma((2, 3)),
             dma((8,)), dma((8,)), dma((16,)), dma((16,)),
         ],
         name="exchange",
-        compiler_params=pltpu.CompilerParams(collective_id=0, has_side_effects=True, vmem_limit_bytes=67043328),
+        compiler_params=pltpu.CompilerParams(collective_id=0, has_side_effects=True, vmem_limit_bytes=54525952),
     )(hist.reshape(4, 4, 2, 2, 96, 128))
 
 
@@ -426,7 +417,7 @@
     mine = local_hist(bin_codes, gradient, hessian, leaf_of_block, block_rows)
     gain, best = exchange(mine)
     split_gain = gain.reshape(2, 4, HI, 4, LO).transpose(0, 1, 3, 2, 4).reshape(2, 16, BINS)
-    return split_gain, best[:2, 0]
+    return split_gain, best[:, 0]
 
 
 def solution(mesh):

time: 67.4 us -> 61.2 us (0.908)
  Pallas kernels: 64.3 us -> 59.1 us
  local copies, waits for them, and re-layouts: 2.9 us -> 1.46 us
    pallas_call x1, Pallas kernels: 37.3 us -> 33.8 us  [exchange(): pl.pallas_call(exchange_kernel, out_shape=(jax.ShapeDtypeStruct((2, 4, HI...]
    pallas_call x1, Pallas kernels: 26.9 us -> 25.3 us  [local_hist(): pl.pallas_call(hist_kernel, out_shape=jax.ShapeDtypeStruct(out, jnp.float...]
    reshape x2, local copies, waits for them, and re-layouts: 1.58 us -> 0.83 us  [local(): gain.reshape(2, 4, HI, 4, LO).transpose(0, 1, 3, 2, 4).reshape(2, 16, BINS)]
    slice x1, local copies, waits for them, and re-layouts: 1.31 us -> 0.63 us  [local(): return (split_gain, best[:, 0])]
where the time goes in v4:
time: 61.2 us; the launch traced here: 61.3 us
  Pallas kernels  59.1 us (97%)
  local copies, waits for them, and re-layouts  1.46 us (2%)
  between operations  0.66 us (1%)
    pallas_call x1, Pallas kernels, exchange(): pl.pallas_call(exchange_kernel, out_shape=(jax.ShapeDtypeStruct((2, 4, HI...  33.8 us
    pallas_call x1, Pallas kernels, local_hist(): pl.pallas_call(hist_kernel, out_shape=jax.ShapeDtypeStruct(out, jnp.float...  25.3 us

profile of v4, /device:TPU:1, one launch (start us, length us, event | category | flops | bytes accessed | tf_op | source)
XLA Modules:
  0.0 61.3 jit_solution(995175507028534625)
XLA Ops:
  0.6 25.3 %histogram.1 = f32[32,2,4,3,8,128]{5,4,3,2,1,0:T(8,128)} custom-call(s32[32]{0:T(128)} %leaf_hbm.1, s32[32]{0:T(128)} %live_hbm.1, s32[4096,512]{1,0:T(8,128)} %codes_hbm.1, bf16[32,128]{1,0:T(8,128)(2,1)} %bitcast.10, bf16[32,128]{1,0:T(8,128)(2,1)} %bitcast.11), custom_call_target="tpu_custom_call" | custom-call | tf_op jit(solution)/shard_map/histogram/pallas_call | solution.py:188
  26.0 33.8 %exchange.1 = (f32[2,4,8,128]{3,2,1,0:T(8,128)S(1)}, f32[2,128]{1,0:T(2,128)S(1)}) custom-call(f32[4,4,2,2,96,128]{5,4,3,2,1,0:T(8,128)} %bitcast.8), custom_call_target="tpu_custom_call" | custom-call | tf_op jit(solution)/shard_map/exchange/pallas_call | solution.py:392
  59.8 0.6 %slice_reduce_fusion = f32[2]{0:T(128)} fusion(f32[2,128]{1,0:T(2,128)S(1)} %get-tuple-element.5), kind=kLoop, calls=%fused_computation | loop fusion | bytes 16 | tf_op jit(solution)/shard_map/slice | solution.py:420
  60.4 0.1 reshape.22
  60.6 0.7 %reshape.23 = f32[2,16,256]{2,1,0:T(8,128)} reshape(f32[2,4,4,8,32]{4,3,2,1,0:T(8,128)S(1)} %copy.8) | data formatting | bytes 65536 | tf_op jit(solution)/shard_map/reshape | solution.py:419
  (1 shorter events, 0.0 us)

commit v5 on v4

--- a/solution.py
+++ b/solution.py
@@ -325,8 +325,10 @@
         first[leaf][1][0].start()
     for leaf in range(2):
         ready(leaf, 1)
+        first[leaf][0][0].wait_send()
         first[leaf][0][1].start()
         ready(leaf, 2)
+        first[leaf][1][0].wait_send()
         first[leaf][1][1].start()
     for leaf in range(2):
         first[leaf][0][0].wait_recv()
@@ -369,19 +371,22 @@
         for copy in copies:
             copy.start()
         for copy in copies:
-            copy.wait()
+            copy.wait_recv()
+        return copies
 
     peak16[0] = top
-    spread(peak16, 16, sb, rb, plane)
+    sent = spread(peak16, 16, sb, rb, plane)
     peak8[0] = jnp.max(peak16[...], 0)
-    spread(peak8, 8, sa, ra, octet)
+    sent += spread(peak8, 8, sa, ra, octet)
     best_ref[...] = jnp.max(peak8[...], 0)
 
+    for copy in sent:
+        copy.wait_send()
     for leaf in range(2):
         for k in range(4):
             pairs[leaf][k].wait_send()
         for way in range(2):
-            for i in range(3):
+            for i in range(1, 3):
                 first[leaf][way][i].wait_send()
         for copy in second[leaf]:
             copy.wait_send()

time: 61.2 us -> 61.3 us (level)
    pallas_call x1, Pallas kernels: 33.8 us -> 31.8 us  [exchange(): pl.pallas_call(exchange_kernel, out_shape=(jax.ShapeDtypeStruct((2, 4, HI...]
    pallas_call x1, Pallas kernels: 25.3 us -> 26.9 us  [local_hist(): pl.pallas_call(hist_kernel, out_shape=jax.ShapeDtypeStruct(out, jnp.float...]
where the time goes in v5:
time: 61.3 us; the launch traced here: 60.8 us
  Pallas kernels  58.7 us (96%)
  local copies, waits for them, and re-layouts  1.46 us (2%)
  between operations  0.66 us (1%)
    pallas_call x1, Pallas kernels, exchange(): pl.pallas_call(exchange_kernel, out_shape=(jax.ShapeDtypeStruct((2, 4, HI...  31.8 us
    pallas_call x1, Pallas kernels, local_hist(): pl.pallas_call(hist_kernel, out_shape=jax.ShapeDtypeStruct(out, jnp.float...  26.9 us

profile of v5, /device:TPU:1, one launch (start us, length us, event | category | flops | bytes accessed | tf_op | source)
XLA Modules:
  0.0 60.8 jit_solution(13455419204383025268)
XLA Ops:
  0.6 26.9 %histogram.1 = f32[32,2,4,3,8,128]{5,4,3,2,1,0:T(8,128)} custom-call(s32[32]{0:T(128)} %leaf_hbm.1, s32[32]{0:T(128)} %live_hbm.1, s32[4096,512]{1,0:T(8,128)} %codes_hbm.1, bf16[32,128]{1,0:T(8,128)(2,1)} %bitcast.10, bf16[32,128]{1,0:T(8,128)(2,1)} %bitcast.11), custom_call_target="tpu_custom_call" | custom-call | tf_op jit(solution)/shard_map/histogram/pallas_call | solution.py:188
  27.6 31.8 %exchange.1 = (f32[2,4,8,128]{3,2,1,0:T(8,128)S(1)}, f32[2,128]{1,0:T(2,128)S(1)}) custom-call(f32[4,4,2,2,96,128]{5,4,3,2,1,0:T(8,128)} %bitcast.8), custom_call_target="tpu_custom_call" | custom-call | tf_op jit(solution)/shard_map/exchange/pallas_call | solution.py:397
  59.4 0.6 %slice_reduce_fusion = f32[2]{0:T(128)} fusion(f32[2,128]{1,0:T(2,128)S(1)} %get-tuple-element.5), kind=kLoop, calls=%fused_computation | loop fusion | bytes 16 | tf_op jit(solution)/shard_map/slice | solution.py:425
  60.0 0.1 reshape.22
  60.1 0.7 %reshape.23 = f32[2,16,256]{2,1,0:T(8,128)} reshape(f32[2,4,4,8,32]{4,3,2,1,0:T(8,128)S(1)} %copy.8) | data formatting | bytes 65536 | tf_op jit(solution)/shard_map/reshape | solution.py:424
  (1 shorter events, 0.0 us)
